TPU v7x, 32 devices: a whole 2x2x4 slice. The times are simulated.
32 devices in a mesh: batch: 8 (over y, x, core), head: 4 (over z).
Axes of the slice: x: 2, y: 2, z: 4, core: 2. Of those that a mesh axis runs over, the one named last changes fastest.
Arguments:
- layer_input: bfloat16 [16384, 768], P(('batch', 'head')), may hold values from -6 to 6
- memory_flags: int32 [32], P('batch'), may hold values 0 or 1
- document_start: int32 [32], P('batch'), may hold values from 1 to 511
- memory_coefficients: bfloat16 [32, 256, 768], P('batch'), may hold values from -6 to 6
- first_gain: bfloat16 [768], replicated, may hold values from 0.5 to 1.5
- first_shift: bfloat16 [768], replicated, may hold values from -1 to 1
- query_weight: bfloat16 [768, 768], P(None, 'head'), may hold values from -0.3125 to 0.3125
- query_bias: bfloat16 [768], P('head'), may hold values from -1 to 1
- key_matrix: bfloat16 [768, 768], P(None, 'head'), may hold values from -0.21875 to 0.21875
- value_matrix: bfloat16 [768, 768], P(None, 'head'), may hold values from -0.21875 to 0.21875
- value_offset_bias: bfloat16 [768], P('head'), may hold values from -1 to 1
- out_weight: bfloat16 [768, 768], P('head'), may hold values from -0.875 to 0.875
- out_bias: bfloat16 [768], replicated, may hold values from -1 to 1
- second_gain: bfloat16 [768], replicated, may hold values from 0.5 to 1.5
- second_shift: bfloat16 [768], replicated, may hold values from -1 to 1
- up_weight: bfloat16 [768, 3072], P(None, 'head'), may hold values from -0.21875 to 0.21875
- up_bias: bfloat16 [3072], P('head'), may hold values from -1 to 1
- down_weight: bfloat16 [3072, 768], P('head'), may hold values from -0.109375 to 0.109375
- down_bias: bfloat16 [768], replicated, may hold values from -1 to 1
- centre_weight: float32 [12, 256], P('head'), may hold values from -0.375 to 0.375
- width_weight: float32 [12, 256], P('head'), may hold values from -0.375 to 0.375
- grad_output: bfloat16 [16384, 768], P(('batch', 'head')), may hold values from -6 to 6
Outputs:
- layer_output: bfloat16 [16384, 768], P(('batch', 'head'))
- input_grad: bfloat16 [16384, 768], P(('batch', 'head'))
- first_gain_grad: float32 [768], replicated
- first_shift_grad: float32 [768], replicated
- query_weight_grad: float32 [768, 768], P(None, 'head')
- query_bias_grad: float32 [768], P('head')
- key_weight_grad: float32 [768, 768], P(None, 'head')
- value_weight_grad: float32 [768, 768], P(None, 'head')
- value_bias_grad: float32 [768], P('head')
- out_weight_grad: float32 [768, 768], P('head')
- out_bias_grad: float32 [768], replicated
- second_gain_grad: float32 [768], replicated
- second_shift_grad: float32 [768], replicated
- up_weight_grad: float32 [768, 3072], P(None, 'head')
- up_bias_grad: float32 [3072], P('head')
- down_weight_grad: float32 [3072, 768], P('head')
- down_bias_grad: float32 [768], replicated
- centre_weight_grad: float32 [12, 256], P('head')
- width_weight_grad: float32 [12, 256], P('head')
Inputs may be any that keep to these rules, and one draw needn't show every extreme that they name: `memory_flags`: 1 marks a segment with memory.
All inputs are finite; a program needn't handle non-finite values. No bound on the sum of `memory_flags` on one device may be relied on, other than what follows from the above.
Results may differ from a plain program's by a relative error of at most 0.018.
The roundings to bfloat16 on the way count: a program that leaves them out, or rounds other values in their place, can miss the bound.
Values may be sent and summed in bfloat16 or wider, within the bound.
A program may use at most 128 MiB of HBM per device.

v0:
```python
import math
import jax
import jax.numpy as jnp
from jax import lax
from jax.sharding import PartitionSpec as P


def norm_stats(values_in):
    center = values_in - jnp.mean(values_in, axis=-1, keepdims=True)
    factor = lax.rsqrt(jnp.mean(center * center, axis=-1, keepdims=True) + 1e-05)
    return (center * factor, factor)


def norm_back(grad, normed, factor):
    return factor * (
        grad
        - jnp.mean(grad, axis=-1, keepdims=True)
        - normed * jnp.mean(grad * normed, axis=-1, keepdims=True)
    )


def cross_dot(left, right):
    return lax.dot_general(
        left, right, (((0,), (0,)), ((), ())), preferred_element_type=jnp.float32
    )


def back_dot(left, right):
    return lax.dot_general(
        left, right, (((1,), (1,)), ((), ())), preferred_element_type=jnp.float32
    )


def segment_mask(length, bound):
    row_ids = lax.broadcasted_iota(jnp.int32, (length, length), 0)
    col_ids = lax.broadcasted_iota(jnp.int32, (length, length), 1)
    return (col_ids <= row_ids) & ((col_ids >= bound) | (row_ids < bound))


def masked_scores(queries, keys_low, bound):
    factor = queries.shape[-1] ** (-0.5)
    scores = (
        jnp.einsum("qhd,khd->hqk", queries, keys_low, preferred_element_type=jnp.float32) * factor
    )
    return jnp.where(segment_mask(queries.shape[0], bound)[None], scores, -1000000000.0)


def recall_terms(queries, memory_keys, centre_weight, width_weight):
    factor = queries.shape[-1] ** (-0.5)
    mem_scores = (
        jnp.einsum("qhd,nhd->hqn", queries, memory_keys, preferred_element_type=jnp.float32)
        * factor
    )
    centre = jax.nn.sigmoid(
        jnp.einsum("hqn,hn->hq", mem_scores, centre_weight, precision=lax.Precision.HIGHEST)
    )
    width_pre = jnp.einsum("hqn,hn->hq", mem_scores, width_weight, precision=lax.Precision.HIGHEST)
    spread = 0.02 * jax.nn.softplus(width_pre) + 0.01
    basis_count = memory_keys.shape[0]
    centres = (jnp.arange(basis_count, dtype=jnp.float32) + 0.5) / basis_count
    offset = centre[..., None] - centres
    recall = (
        jnp.exp(-offset * offset / (2.0 * spread[..., None]))
        * lax.rsqrt(2.0 * math.pi * spread[..., None])
        / basis_count
    )
    return (mem_scores, centre, width_pre, spread, offset, recall)


def forward_segment(segment_item, centre_weight, width_weight):
    queries, keys_low, values, memory_keys, memory_values, flag, bound = segment_item
    scores = masked_scores(queries, keys_low, bound)
    row_peak = jnp.max(scores, axis=-1, keepdims=True)
    shifted = jnp.exp(scores - row_peak)
    row_total = jnp.sum(shifted, axis=-1, keepdims=True)
    probs_low = (shifted / row_total).astype(jnp.bfloat16)
    local_mix = jnp.einsum("hqk,khd->qhd", probs_low, values, preferred_element_type=jnp.float32)
    recall_low = recall_terms(queries, memory_keys, centre_weight, width_weight)[5].astype(
        jnp.bfloat16
    )
    recalled = jnp.einsum(
        "hqn,nhd->qhd", recall_low, memory_values, preferred_element_type=jnp.float32
    )
    context = (local_mix + flag * recalled).astype(jnp.bfloat16)
    return (context, (row_peak + jnp.log(row_total))[..., 0])


def backward_segment(segment_item, centre_weight, width_weight):
    queries, keys_low, values, memory_keys, memory_values, flag, bound, log_total, grad_context = (
        segment_item
    )
    factor = queries.shape[-1] ** (-0.5)
    scores = masked_scores(queries, keys_low, bound)
    attn_probs = jnp.exp(scores - log_total[..., None])
    probs_low = attn_probs.astype(jnp.bfloat16)
    grad_values = jnp.einsum(
        "hqk,qhd->khd", probs_low, grad_context, preferred_element_type=jnp.float32
    )
    grad_probs = jnp.einsum(
        "qhd,khd->hqk", grad_context, values, preferred_element_type=jnp.float32
    )
    grad_scores = (
        attn_probs * (grad_probs - jnp.sum(attn_probs * grad_probs, axis=-1, keepdims=True))
    ).astype(jnp.bfloat16)
    mem_scores, centre, width_pre, spread, offset, recall = recall_terms(
        queries, memory_keys, centre_weight, width_weight
    )
    recall_low = recall.astype(jnp.bfloat16)
    grad_recall = flag * jnp.einsum(
        "qhd,nhd->hqn", grad_context, memory_values, preferred_element_type=jnp.float32
    )
    memory_value_gradient = flag * jnp.einsum(
        "hqn,qhd->nhd", recall_low, grad_context, preferred_element_type=jnp.float32
    )
    weighted = grad_recall * recall
    spread_b = spread[..., None]
    grad_centre = jnp.sum(weighted * (-offset / spread_b), axis=-1)
    grad_spread = jnp.sum(
        weighted * (offset * offset / (2.0 * spread_b * spread_b) - 0.5 / spread_b), axis=-1
    )
    centre_pre_grad = grad_centre * centre * (1.0 - centre)
    width_pre_grad = grad_spread * 0.02 * jax.nn.sigmoid(width_pre)
    grad_mem_scores = (
        centre_pre_grad[..., None] * centre_weight[:, None, :]
        + width_pre_grad[..., None] * width_weight[:, None, :]
    ).astype(jnp.bfloat16)
    centre_grad = jnp.einsum(
        "hq,hqn->hn", centre_pre_grad, mem_scores, precision=lax.Precision.HIGHEST
    )
    width_grad = jnp.einsum(
        "hq,hqn->hn", width_pre_grad, mem_scores, precision=lax.Precision.HIGHEST
    )
    grad_queries = factor * (
        jnp.einsum("hqk,khd->qhd", grad_scores, keys_low, preferred_element_type=jnp.float32)
        + jnp.einsum(
            "hqn,nhd->qhd", grad_mem_scores, memory_keys, preferred_element_type=jnp.float32
        )
    )
    grad_keys = factor * jnp.einsum(
        "hqk,qhd->khd", grad_scores, queries, preferred_element_type=jnp.float32
    )
    memory_key_gradient = factor * jnp.einsum(
        "hqn,qhd->nhd", grad_mem_scores, queries, preferred_element_type=jnp.float32
    )
    return (
        grad_queries.astype(jnp.bfloat16),
        grad_keys.astype(jnp.bfloat16),
        grad_values.astype(jnp.bfloat16),
        memory_key_gradient.astype(jnp.bfloat16),
        memory_value_gradient.astype(jnp.bfloat16),
        centre_grad,
        width_grad,
    )


def per_device(
    layer_input,
    memory_flags,
    document_start,
    memory_coefficients,
    first_gain,
    first_shift,
    query_weight,
    query_bias,
    key_matrix,
    value_matrix,
    value_offset_bias,
    out_weight,
    out_bias,
    second_gain,
    second_shift,
    up_weight,
    up_bias,
    down_weight,
    down_bias,
    centre_weight,
    width_weight,
    grad_output,
):
    segments = memory_coefficients.shape[0]
    basis_count = memory_coefficients.shape[1]
    group_heads = centre_weight.shape[0]
    group_cols = query_weight.shape[1]
    head_size = group_cols // group_heads
    flag_values = memory_flags.astype(jnp.float32)
    inputs = layer_input.astype(jnp.float32)
    normed_one, factor_one = norm_stats(inputs)
    first_low = (normed_one * first_gain + first_shift).astype(jnp.bfloat16)
    first_rows = lax.all_gather(first_low, "head", axis=0, tiled=True)
    total_rows = first_rows.shape[0]
    length = total_rows // segments
    queries = (
        jnp.dot(first_rows, query_weight, preferred_element_type=jnp.float32) + query_bias
    ).astype(jnp.bfloat16)
    keys_low = jnp.dot(first_rows, key_matrix, preferred_element_type=jnp.float32).astype(
        jnp.bfloat16
    )
    values = (
        jnp.dot(first_rows, value_matrix, preferred_element_type=jnp.float32) + value_offset_bias
    ).astype(jnp.bfloat16)
    memory_keys = jnp.einsum(
        "wmr,rq->wmq", memory_coefficients, key_matrix, preferred_element_type=jnp.float32
    ).astype(jnp.bfloat16)
    memory_values = (
        jnp.einsum(
            "wmr,rq->wmq", memory_coefficients, value_matrix, preferred_element_type=jnp.float32
        )
        + value_offset_bias
    ).astype(jnp.bfloat16)
    tile_shape = (segments, length, group_heads, head_size)
    basis_dimensions = (segments, basis_count, group_heads, head_size)
    seg_items = (
        queries.reshape(tile_shape),
        keys_low.reshape(tile_shape),
        values.reshape(tile_shape),
        memory_keys.reshape(basis_dimensions),
        memory_values.reshape(basis_dimensions),
        flag_values,
        document_start,
    )
    context, log_total = lax.map(
        lambda segment_item: forward_segment(segment_item, centre_weight, width_weight), seg_items
    )
    context = context.reshape(total_rows, group_cols)
    attn_sum = lax.psum_scatter(
        jnp.dot(context, out_weight, preferred_element_type=jnp.float32).astype(jnp.bfloat16),
        "head",
        scatter_dimension=0,
        tiled=True,
    ).astype(jnp.float32)
    hidden = inputs + (attn_sum + out_bias)
    normed_two, factor_two = norm_stats(hidden)
    second_low = (normed_two * second_gain + second_shift).astype(jnp.bfloat16)
    second_rows = lax.all_gather(second_low, "head", axis=0, tiled=True)
    up_pre = jnp.dot(second_rows, up_weight, preferred_element_type=jnp.float32) + up_bias
    up_act = jax.nn.gelu(up_pre, approximate=True).astype(jnp.bfloat16)
    mlp_sum = lax.psum_scatter(
        jnp.dot(up_act, down_weight, preferred_element_type=jnp.float32).astype(jnp.bfloat16),
        "head",
        scatter_dimension=0,
        tiled=True,
    ).astype(jnp.float32)
    layer_output = (hidden + (mlp_sum + down_bias)).astype(jnp.bfloat16)
    down_bias_grad = jnp.sum(grad_output.astype(jnp.float32), axis=0)
    grad_rows = lax.all_gather(grad_output, "head", axis=0, tiled=True)
    down_weight_grad = cross_dot(up_act, grad_rows)
    grad_act = back_dot(grad_rows, down_weight)
    gelu_pull = jax.vjp(lambda values_in: jax.nn.gelu(values_in, approximate=True), up_pre)[1]
    grad_up = gelu_pull(grad_act)[0].astype(jnp.bfloat16)
    up_bias_grad = jnp.sum(grad_up.astype(jnp.float32), axis=0)
    up_weight_grad = cross_dot(second_rows, grad_up)
    grad_second = lax.psum_scatter(
        back_dot(grad_up, up_weight).astype(jnp.bfloat16), "head", scatter_dimension=0, tiled=True
    ).astype(jnp.float32)
    second_gain_grad = jnp.sum(grad_second * normed_two, axis=0)
    second_shift_grad = jnp.sum(grad_second, axis=0)
    grad_hidden = grad_output.astype(jnp.float32) + norm_back(
        grad_second * second_gain, normed_two, factor_two
    )
    branch_low = grad_hidden.astype(jnp.bfloat16)
    out_bias_grad = jnp.sum(branch_low.astype(jnp.float32), axis=0)
    branch_rows = lax.all_gather(branch_low, "head", axis=0, tiled=True)
    out_weight_grad = cross_dot(context, branch_rows)
    grad_context = back_dot(branch_rows, out_weight).astype(jnp.bfloat16)
    back_items = seg_items + (log_total, grad_context.reshape(tile_shape))
    results = lax.map(
        lambda segment_item: backward_segment(segment_item, centre_weight, width_weight), back_items
    )
    grad_queries = results[0].reshape(total_rows, group_cols)
    grad_keys = results[1].reshape(total_rows, group_cols)
    grad_values = results[2].reshape(total_rows, group_cols)
    memory_key_gradient = results[3].reshape(segments, basis_count, group_cols)
    memory_value_gradient = results[4].reshape(segments, basis_count, group_cols)
    centre_weight_grad = jnp.sum(results[5], axis=0)
    width_weight_grad = jnp.sum(results[6], axis=0)
    query_weight_grad = cross_dot(first_rows, grad_queries)
    query_bias_grad = jnp.sum(grad_queries.astype(jnp.float32), axis=0)
    key_weight_grad = cross_dot(first_rows, grad_keys) + jnp.einsum(
        "qwo,qwy->oy", memory_coefficients, memory_key_gradient, preferred_element_type=jnp.float32
    )
    value_weight_grad = cross_dot(first_rows, grad_values) + jnp.einsum(
        "qwo,qwy->oy",
        memory_coefficients,
        memory_value_gradient,
        preferred_element_type=jnp.float32,
    )
    value_bias_grad = jnp.sum(grad_values.astype(jnp.float32), axis=0) + jnp.sum(
        memory_value_gradient.astype(jnp.float32), axis=(0, 1)
    )
    grad_first = lax.psum_scatter(
        (
            back_dot(grad_queries, query_weight)
            + back_dot(grad_keys, key_matrix)
            + back_dot(grad_values, value_matrix)
        ).astype(jnp.bfloat16),
        "head",
        scatter_dimension=0,
        tiled=True,
    ).astype(jnp.float32)
    first_gain_grad = jnp.sum(grad_first * normed_one, axis=0)
    first_shift_grad = jnp.sum(grad_first, axis=0)
    input_grad = (grad_hidden + norm_back(grad_first * first_gain, normed_one, factor_one)).astype(
        jnp.bfloat16
    )
    (
        query_weight_grad,
        query_bias_grad,
        key_weight_grad,
        value_weight_grad,
        value_bias_grad,
        out_weight_grad,
        centre_weight_grad,
        width_weight_grad,
        down_weight_grad,
        up_weight_grad,
        up_bias_grad,
    ) = lax.psum(
        (
            query_weight_grad,
            query_bias_grad,
            key_weight_grad,
            value_weight_grad,
            value_bias_grad,
            out_weight_grad,
            centre_weight_grad,
            width_weight_grad,
            down_weight_grad,
            up_weight_grad,
            up_bias_grad,
        ),
        "batch",
    )
    (
        first_gain_grad,
        first_shift_grad,
        out_bias_grad,
        second_gain_grad,
        second_shift_grad,
        down_bias_grad,
    ) = lax.psum(
        (
            first_gain_grad,
            first_shift_grad,
            out_bias_grad,
            second_gain_grad,
            second_shift_grad,
            down_bias_grad,
        ),
        ("batch", "head"),
    )
    return (
        layer_output,
        input_grad,
        first_gain_grad,
        first_shift_grad,
        query_weight_grad,
        query_bias_grad,
        key_weight_grad,
        value_weight_grad,
        value_bias_grad,
        out_weight_grad,
        out_bias_grad,
        second_gain_grad,
        second_shift_grad,
        up_weight_grad,
        up_bias_grad,
        down_weight_grad,
        down_bias_grad,
        centre_weight_grad,
        width_weight_grad,
    )


def solution(mesh):
    placed = (
        P(("batch", "head"), None),
        P("batch"),
        P("batch"),
        P("batch", None, None),
        P(),
        P(),
        P(None, "head"),
        P("head"),
        P(None, "head"),
        P(None, "head"),
        P("head"),
        P("head", None),
        P(),
        P(),
        P(),
        P(None, "head"),
        P("head"),
        P("head", None),
        P(),
        P("head", None),
        P("head", None),
        P(("batch", "head"), None),
    )
    return jax.shard_map(
        per_device,
        mesh=mesh,
        in_specs=placed,
        out_specs=(
            P(("batch", "head"), None),
            P(("batch", "head"), None),
            P(),
            P(),
            P(None, "head"),
            P("head"),
            P(None, "head"),
            P(None, "head"),
            P("head"),
            P("head", None),
            P(),
            P(),
            P(),
            P(None, "head"),
            P("head"),
            P("head", None),
            P(),
            P("head", None),
            P("head", None),
        ),
        check_vma=False,
    )
```

profile of v0, /device:TPU:0, one launch (start us, length us, event | category | flops | bytes accessed | tf_op | source)
XLA Modules:
  0.0 868.7 jit_solution(15008076573527793442)
XLA Ops:
  14.6 64.0 %all-gather.5.cloned.1.call-done = bf16[2048,768]{1,0:T(8,128)(2,1)} async-done(((bf16[512,768]{1,0:T(8,128)(2,1)}), bf16[2048,768]{1,0:T(8,128)(2,1)}) %all-gather.5.cloned.1.call-update) | async-done | bytes 3145744 | tf_op jit(solution)/shard_map/all_gather | solution.py:189
  78.6 3.1 fusion.166
  84.5 3.9 fusion.165
  88.4 3.1 reshape.257
  93.7 4.0 convolution_convert_fusion.4
  97.7 3.0 reshape.259
  103.9 54.4 %while.34 = (s32[]{:T(128)}, bf16[4,512,3,64]{1,3,2,0:T(8,128)(2,1)}, f32[4,3,512]{2,1,0:T(4,128)}, bf16[4,512,3,64]{1,3,2,0:T(8,128)(2,1)}, s32[4]{0:T(128)S(1)...) while((s32[]{:T(128)}, ...), condition=%wide.region_5.6_spmd, body=%wide.region_2.5_spmd.sunk | while | flops 325111296 | bytes 17297064 | solution.py:221
  114.3 3.2 fusion.321
  127.9 3.2 fusion.321
  141.5 3.2 fusion.321
  155.0 3.2 fusion.321
  166.4 56.4 %reduce-scatter.5.cloned.1.call-done = bf16[512,768]{1,0:T(8,128)(2,1)} async-done(((bf16[2048,768]{1,0:T(8,128)(2,1)}), bf16[512,768]{1,0:T(8,128)(2,1)}) %reduce-scatter.5.cloned.1.call-update) | async-done | bytes 786448 | tf_op jit(solution)/shard_map/reduce_scatter | solution.py:225
  228.9 61.8 %all-gather.7.cloned.1.call-done = bf16[2048,768]{1,0:T(8,128)(2,1)} async-done(((bf16[512,768]{1,0:T(8,128)(2,1)}), bf16[2048,768]{1,0:T(8,128)(2,1)}) %all-gather.7.cloned.1.call-update) | async-done | bytes 3145744 | tf_op jit(solution)/shard_map/all_gather | solution.py:234
  290.6 7.5 fusion.196
  298.1 56.1 %all-gather.9.cloned.1.call-done = bf16[2048,768]{1,0:T(8,128)(2,1)} async-done(((bf16[512,768]{1,0:T(8,128)(2,1)}), bf16[2048,768]{1,0:T(8,128)(2,1)}) %all-gather.9.cloned.1.call-update) | async-done | bytes 3145744 | tf_op jit(solution)/shard_map/all_gather | solution.py:245
  354.3 11.0 %convert_reduce_fusion = (f32[768]{0:T(1024)}, bf16[2048,768]{1,0:T(8,128)(2,1)S(1)}, bf16[2048,768]{1,0:T(8,128)(2,1)}) fusion(f32[2048,768]{1,0:T(8,128)} %fusion.196, f32[768]{0:T(1024)} %convert_element_type.193, bf16[2048,768]{1,0:T(8,128)(2,1)} %all-gather.9.cloned.1.call-done, bf16[768,768]{1,0:T(8,128)(2,1)} %param.43), kind=kOutput, calls=%fused_computation.206 | convolution fusion | flops 2455239936 | bytes 16914432 | tf_op jit(solution)/shard_map/dot_general | solution.py:29
  366.9 4.0 convolution_convert_fusion
  371.0 6.5 convolution_convert_fusion.1
  378.8 51.2 %reduce-scatter.9.cloned.1.call-done = bf16[512,768]{1,0:T(8,128)(2,1)} async-done(((bf16[2048,768]{1,0:T(8,128)(2,1)}), bf16[512,768]{1,0:T(8,128)(2,1)}) %reduce-scatter.9.cloned.1.call-update) | async-done | bytes 786448 | tf_op jit(solution)/shard_map/reduce_scatter | solution.py:252
  430.0 2.9 fusion.188
  433.5 59.0 %reduce-scatter.7.cloned.1.call-done = bf16[512,768]{1,0:T(8,128)(2,1)} async-done(((bf16[2048,768]{1,0:T(8,128)(2,1)}), bf16[512,768]{1,0:T(8,128)(2,1)}) %reduce-scatter.7.cloned.1.call-update) | async-done | bytes 786448 | tf_op jit(solution)/shard_map/reduce_scatter | solution.py:237
  492.5 5.3 convert_reduce_fusion.5
  497.8 63.6 %all-gather.11.cloned.1.call-done = bf16[2048,768]{1,0:T(8,128)(2,1)} async-done(((bf16[512,768]{1,0:T(8,128)(2,1)}), bf16[2048,768]{1,0:T(8,128)(2,1)}) %all-gather.11.cloned.1.call-update) | async-done | bytes 3145744 | tf_op jit(solution)/shard_map/all_gather | solution.py:262
  561.4 4.0 convolution_convert_fusion.3
  565.4 3.4 reshape.263
  573.9 91.2 %while.35 = (s32[]{:T(128)}, bf16[4,512,3,64]{1,3,2,0:T(8,128)(2,1)}, bf16[4,512,3,64]{1,3,2,0:T(8,128)(2,1)}, bf16[4,512,3,64]{1,3,2,0:T(8,128)(2,1)}, bf16[4,2...) while((s32[]{:T(128)}, ...), condition=%wide.region_17.18_spmd, body=%wide.region_13.17_spmd.sunk | while | flops 795121152 | bytes 42630428 | solution.py:266
  674.6 7.1 fusion.201
  681.7 4.2 fusion.200
  701.8 25.6 %all-reduce.1 = (f32[192]{0:T(256)}, f32[192]{0:T(256)}, f32[768]{0:T(1024)}, f32[3,256]{1,0:T(4,128)}, f32[3,256]{1,0:T(4,128)}) all-reduce(f32[192]{0:T(256)} %reduce_sum.229, f32[192]{0:T(256)S(1)} %add.258, f32[768]{0:T(1024)} %get-tuple-element.347, f32[3,256]{1,0:T(4,128)} %reduce_sum.237, ...), channel_id=1, replica_groups=mesh['batch'=8,'head'=4] {'batch'}, use_global_device_ids=true, to_apply=%region_27.28 | all-reduce | flops 2688 | bytes 21504 | tf_op jit(solution)/shard_map/psum | solution.py:317
  727.4 6.2 reduce-scatter.11.cloned.1.call-done
  735.7 41.8 %all-reduce = (f32[768]{0:T(1024)}, f32[768]{0:T(1024)}, f32[768]{0:T(1024)}, f32[768]{0:T(1024)}, f32[768]{0:T(1024)}, /*index=5*/f32[768]{0:T(1024)}) all-reduce(f32[768]{0:T(1024)S(1)} %get-tuple-element.260, f32[768]{0:T(1024)S(1)} %get-tuple-element.265, ...), channel_id=1, replica_groups=mesh['batch'=8,'head'=4] {'batch','head'}, use_global_device_ids=true, to_apply=%region_22.23 | all-reduce | flops 4608 | bytes 36864 | tf_op jit(solution)/shard_map/psum | solution.py:340
  780.4 73.2 %all-reduce.5.cloned.1.call-done = (f32[768,192]{0,1:T(8,128)}, f32[768,192]{0,1:T(8,128)}, f32[768,192]{0,1:T(8,128)}, f32[192,768]{1,0:T(8,128)}, f32[768,768]{1,0:T(8,128)}, /*index=5*/f32[768,768]{1,0:T(8,128)}) async-done(((f32[768,192]{0,1:T(8,128)}, f32[768,192]{0,1:T(8,128)}, f32[768,192]{0,1:T(8,128)}, f32[192,768]{1,0:T(8,128)}, f32[768,768]{1,0:T(8,128)}, /*index=5*/f32[768,768]{1,0:T(8,128)}), ...) | async-done | bytes 7077904 | tf_op jit(solution)/shard_map/psum | solution.py:317
  (381 shorter events, 208.5 us)
Async XLA Ops:
  7.2 5.2 copy-start
  7.2 3.8 copy-start.1
  7.2 3.2 copy-start.46
  7.2 71.4 %all-gather.5.cloned.1.call-start = ((), (), s32[]{:S(2)}) async-start(), calls=%async_computation.4 | async-start | bytes 3932160 | tf_op jit(solution)/shard_map/all_gather | solution.py:189
  8.8 3.6 copy-start.50
  8.8 3.6 copy-start.51
  8.8 3.6 copy-start.52
  8.8 3.6 copy-start.26
  12.3 210.6 %reduce-scatter.5.cloned.1.call-start = ((), (), s32[]{:S(2)}) async-start(), calls=%async_computation.5 | async-start | bytes 3932160 | tf_op jit(solution)/shard_map/reduce_scatter | solution.py:225
  100.7 3.2 copy-start.33
  100.7 3.2 copy-start.34
  100.7 3.2 copy-start.53
  163.8 126.8 %all-gather.7.cloned.1.call-start = ((), (), s32[]{:S(2)}) async-start(), calls=%async_computation.6 | async-start | bytes 3932160 | tf_op jit(solution)/shard_map/all_gather | solution.py:234
  227.0 127.3 %all-gather.9.cloned.1.call-start = ((), (), s32[]{:S(2)}) async-start(), calls=%async_computation.8 | async-start | bytes 3932160 | tf_op jit(solution)/shard_map/all_gather | solution.py:245
  227.6 202.4 %reduce-scatter.9.cloned.1.call-start = ((), (), s32[]{:S(2)}) async-start(), calls=%async_computation.9 | async-start | bytes 3932160 | tf_op jit(solution)/shard_map/reduce_scatter | solution.py:252
  354.3 12.6 %copy-start.49 = (bf16[768,768]{1,0:T(8,128)(2,1)S(1)}, bf16[768,768]{1,0:T(8,128)(2,1)}, u32[]{:S(2)}) copy-start(bf16[768,768]{1,0:T(8,128)(2,1)} %param.41) | copy-start | bytes 3538948
  370.9 121.5 %reduce-scatter.7.cloned.1.call-start = ((), (), s32[]{:S(2)}) async-start(), calls=%async_computation.7 | async-start | bytes 3932160 | tf_op jit(solution)/shard_map/reduce_scatter | solution.py:237
  377.5 183.9 %all-gather.11.cloned.1.call-start = ((), (), s32[]{:S(2)}) async-start(), calls=%async_computation.10 | async-start | bytes 3932160 | tf_op jit(solution)/shard_map/all_gather | solution.py:262
  497.8 235.9 %reduce-scatter.11.cloned.1.call-start = ((), (), s32[]{:S(2)}) async-start(), calls=%async_computation.11 | async-start | bytes 3932160 | tf_op jit(solution)/shard_map/reduce_scatter | solution.py:290
  667.2 3.5 copy-start.9
  668.0 3.7 copy-start.12
  674.5 179.0 %all-reduce.5.cloned.1.call-start = ((), (), s32[]{:S(2)}) async-start(), calls=%async_computation.12 | async-start | bytes 14155776 | tf_op jit(solution)/shard_map/psum | solution.py:317
  674.6 7.1 copy-start.48
  674.6 7.1 copy-start.58
  681.7 4.2 copy-start.25
  695.3 6.1 copy-start.15
  695.3 38.3 %copy-start.36 = (f32[768]{0:T(1024)S(1)}, f32[768]{0:T(1024)}, u32[]{:S(2)}) copy-start(f32[768]{0:T(1024)} %copy-done.35) | copy-start | bytes 9220
  695.4 38.3 %copy-start.38 = (f32[512]{0:T(512)S(1)}, f32[512]{0:T(512)}, u32[]{:S(2)}) copy-start(f32[512]{0:T(512)} %copy-done.37) | copy-start | bytes 6148
  695.4 38.3 %copy-start.41 = (f32[512]{0:T(512)S(1)}, f32[512]{0:T(512)}, u32[]{:S(2)}) copy-start(f32[512]{0:T(512)} %copy-done.40) | copy-start | bytes 6148
  700.0 35.7 %copy-start.44 = (f32[768]{0:T(1024)S(1)}, f32[768]{0:T(1024)}, u32[]{:S(2)}) copy-start(f32[768]{0:T(1024)} %get-tuple-element.258) | copy-start | bytes 9220
  733.6 43.9 %copy-start.18 = (bf16[512,768]{1,0:T(8,128)(2,1)S(1)}, bf16[512,768]{1,0:T(8,128)(2,1)}, u32[]{:S(2)}) copy-start(bf16[512,768]{1,0:T(8,128)(2,1)} %reduce-scatter.11.cloned.1.call-done) | copy-start | bytes 2359300
  853.5 3.7 copy-start.22
  (42 other events, 76.2 us)
Sparse Core Ops, SparseCore 0:
  12.4 66.1 all-gather.4
  163.9 58.8 reduce-scatter.4
  227.1 63.5 all-gather.6
  292.1 62.1 all-gather.8
  371.0 58.8 reduce-scatter.8
  432.1 60.2 reduce-scatter.6
  497.9 63.5 all-gather.10
  674.7 58.8 reduce-scatter.10
  738.8 114.6 all-reduce.4
where the time goes:
time: 874 us; the launch traced here: 869 us
  waiting for transfers between devices  492 us (56%)
  matrix products  186 us (21%)
  blocking collectives  67.4 us (8%)
  local copies, waits for them, and re-layouts  60 us (7%)
  other arithmetic  46.6 us (5%)
  between operations  14.6 us (2%)
    psum x1, waiting for transfers between devices, per_device(): lax.psum((query_weight_grad, query_bias_grad, key_weight_grad, value_weig...  73.2 us
    all_gather x1, waiting for transfers between devices, per_device(): first_rows = lax.all_gather(first_low, 'head', axis=0, tiled=True)  64 us
    all_gather x1, waiting for transfers between devices, per_device(): branch_rows = lax.all_gather(branch_low, 'head', axis=0, tiled=True)  63.6 us
    all_gather x1, waiting for transfers between devices, per_device(): second_rows = lax.all_gather(second_low, 'head', axis=0, tiled=True)  61.8 us
    reduce_scatter x1, waiting for transfers between devices, per_device(): lax.psum_scatter(jnp.dot(up_act, down_weight, preferred_element_type=jnp....  59 us
    reduce_scatter x1, waiting for transfers between devices, per_device(): lax.psum_scatter(jnp.dot(context, out_weight, preferred_element_type=jnp....  56.4 us
    all_gather x1, waiting for transfers between devices, per_device(): grad_rows = lax.all_gather(grad_output, 'head', axis=0, tiled=True)  56.1 us
    reduce_scatter x1, waiting for transfers between devices, per_device(): lax.psum_scatter(back_dot(grad_up, up_weight).astype(jnp.bfloat16), 'head...  51.2 us
  transfers between devices with their start and end apart: 9, of which 9 were waited for; matrix products, arithmetic and copies ran while one was open for 6% of the time, Pallas kernels for 0%

commit v1 on v0

--- a/solution.py
+++ b/solution.py
@@ -338,15 +338,18 @@
         second_shift_grad,
         down_bias_grad,
     ) = lax.psum(
-        (
-            first_gain_grad,
-            first_shift_grad,
-            out_bias_grad,
-            second_gain_grad,
-            second_shift_grad,
-            down_bias_grad,
+        lax.psum(
+            (
+                first_gain_grad,
+                first_shift_grad,
+                out_bias_grad,
+                second_gain_grad,
+                second_shift_grad,
+                down_bias_grad,
+            ),
+            "head",
         ),
-        ("batch", "head"),
+        "batch",
     )
     return (
         layer_output,

time: 874 us -> 874 us (level)
  waiting for transfers between devices: 492 us -> 516 us
  blocking collectives: 67.4 us -> 44.2 us
    reduce_scatter x1, waiting for transfers between devices: 6.24 us -> 31.8 us  [per_device(): lax.psum_scatter((back_dot(grad_queries, query_weight) + back_dot(grad_ke...]
    psum x1, blocking collectives: 41.8 us -> 18.4 us  [per_device(): lax.psum((first_gain_grad, first_shift_grad, out_bias_grad, second_gain_g...]
where the time goes in v1:
time: 874 us; the launch traced here: 869 us
  waiting for transfers between devices  516 us (59%)
  matrix products  186 us (21%)
  local copies, waits for them, and re-layouts  60 us (7%)
  other arithmetic  46.6 us (5%)
  blocking collectives  44.2 us (5%)
  between operations  14.7 us (2%)
    psum x1, waiting for transfers between devices, per_device(): lax.psum((query_weight_grad, query_bias_grad, key_weight_grad, value_weig...  71.1 us
    all_gather x1, waiting for transfers between devices, per_device(): first_rows = lax.all_gather(first_low, 'head', axis=0, tiled=True)  64 us
    all_gather x1, waiting for transfers between devices, per_device(): branch_rows = lax.all_gather(branch_low, 'head', axis=0, tiled=True)  63.6 us
    all_gather x1, waiting for transfers between devices, per_device(): second_rows = lax.all_gather(second_low, 'head', axis=0, tiled=True)  61.8 us
    reduce_scatter x1, waiting for transfers between devices, per_device(): lax.psum_scatter(jnp.dot(up_act, down_weight, preferred_element_type=jnp....  59 us
    reduce_scatter x1, waiting for transfers between devices, per_device(): lax.psum_scatter(jnp.dot(context, out_weight, preferred_element_type=jnp....  56.4 us
    all_gather x1, waiting for transfers between devices, per_device(): grad_rows = lax.all_gather(grad_output, 'head', axis=0, tiled=True)  56.1 us
    reduce_scatter x1, waiting for transfers between devices, per_device(): lax.psum_scatter(back_dot(grad_up, up_weight).astype(jnp.bfloat16), 'head...  51.2 us
  transfers between devices with their start and end apart: 9, of which 9 were waited for; matrix products, arithmetic and copies ran while one was open for 6% of the time, Pallas kernels for 0%

profile of v1, /device:TPU:0, one launch (start us, length us, event | category | flops | bytes accessed | tf_op | source)
XLA Modules:
  0.0 868.9 jit_solution(14680006970240782889)
XLA Ops:
  14.6 64.0 %all-gather.5.cloned.1.call-done = bf16[2048,768]{1,0:T(8,128)(2,1)} async-done(((bf16[512,768]{1,0:T(8,128)(2,1)}), bf16[2048,768]{1,0:T(8,128)(2,1)}) %all-gather.5.cloned.1.call-update) | async-done | bytes 3145744 | tf_op jit(solution)/shard_map/all_gather | solution.py:189
  78.6 3.1 fusion.166
  84.5 3.9 fusion.165
  88.4 3.1 reshape.257
  93.7 4.0 convolution_convert_fusion.4
  97.7 3.0 reshape.259
  103.9 54.4 %while.34 = (s32[]{:T(128)}, bf16[4,512,3,64]{1,3,2,0:T(8,128)(2,1)}, f32[4,3,512]{2,1,0:T(4,128)}, bf16[4,512,3,64]{1,3,2,0:T(8,128)(2,1)}, s32[4]{0:T(128)S(1)...) while((s32[]{:T(128)}, ...), condition=%wide.region_5.6_spmd, body=%wide.region_2.5_spmd.sunk | while | flops 325111296 | bytes 17297064 | solution.py:221
  114.3 3.2 fusion.321
  127.9 3.2 fusion.321
  141.5 3.2 fusion.321
  155.0 3.2 fusion.321
  166.5 56.4 %reduce-scatter.5.cloned.1.call-done = bf16[512,768]{1,0:T(8,128)(2,1)} async-done(((bf16[2048,768]{1,0:T(8,128)(2,1)}), bf16[512,768]{1,0:T(8,128)(2,1)}) %reduce-scatter.5.cloned.1.call-update) | async-done | bytes 786448 | tf_op jit(solution)/shard_map/reduce_scatter | solution.py:225
  228.9 61.8 %all-gather.7.cloned.1.call-done = bf16[2048,768]{1,0:T(8,128)(2,1)} async-done(((bf16[512,768]{1,0:T(8,128)(2,1)}), bf16[2048,768]{1,0:T(8,128)(2,1)}) %all-gather.7.cloned.1.call-update) | async-done | bytes 3145744 | tf_op jit(solution)/shard_map/all_gather | solution.py:234
  290.7 7.5 fusion.196
  298.2 56.1 %all-gather.9.cloned.1.call-done = bf16[2048,768]{1,0:T(8,128)(2,1)} async-done(((bf16[512,768]{1,0:T(8,128)(2,1)}), bf16[2048,768]{1,0:T(8,128)(2,1)}) %all-gather.9.cloned.1.call-update) | async-done | bytes 3145744 | tf_op jit(solution)/shard_map/all_gather | solution.py:245
  354.3 11.0 %convert_reduce_fusion = (f32[768]{0:T(1024)}, bf16[2048,768]{1,0:T(8,128)(2,1)S(1)}, bf16[2048,768]{1,0:T(8,128)(2,1)}) fusion(f32[2048,768]{1,0:T(8,128)} %fusion.196, f32[768]{0:T(1024)} %convert_element_type.193, bf16[2048,768]{1,0:T(8,128)(2,1)} %all-gather.9.cloned.1.call-done, bf16[768,768]{1,0:T(8,128)(2,1)} %param.43), kind=kOutput, calls=%fused_computation.206 | convolution fusion | flops 2455239936 | bytes 16914432 | tf_op jit(solution)/shard_map/dot_general | solution.py:29
  366.9 4.0 convolution_convert_fusion
  371.0 6.5 convolution_convert_fusion.1
  378.8 51.2 %reduce-scatter.9.cloned.1.call-done = bf16[512,768]{1,0:T(8,128)(2,1)} async-done(((bf16[2048,768]{1,0:T(8,128)(2,1)}), bf16[512,768]{1,0:T(8,128)(2,1)}) %reduce-scatter.9.cloned.1.call-update) | async-done | bytes 786448 | tf_op jit(solution)/shard_map/reduce_scatter | solution.py:252
  430.0 2.9 fusion.188
  433.5 59.0 %reduce-scatter.7.cloned.1.call-done = bf16[512,768]{1,0:T(8,128)(2,1)} async-done(((bf16[2048,768]{1,0:T(8,128)(2,1)}), bf16[512,768]{1,0:T(8,128)(2,1)}) %reduce-scatter.7.cloned.1.call-update) | async-done | bytes 786448 | tf_op jit(solution)/shard_map/reduce_scatter | solution.py:237
  492.5 5.3 convert_reduce_fusion.5
  497.9 63.6 %all-gather.11.cloned.1.call-done = bf16[2048,768]{1,0:T(8,128)(2,1)} async-done(((bf16[512,768]{1,0:T(8,128)(2,1)}), bf16[2048,768]{1,0:T(8,128)(2,1)}) %all-gather.11.cloned.1.call-update) | async-done | bytes 3145744 | tf_op jit(solution)/shard_map/all_gather | solution.py:262
  561.4 4.0 convolution_convert_fusion.3
  565.4 3.4 reshape.263
  573.9 91.2 %while.35 = (s32[]{:T(128)}, bf16[4,512,3,64]{1,3,2,0:T(8,128)(2,1)}, bf16[4,512,3,64]{1,3,2,0:T(8,128)(2,1)}, bf16[4,512,3,64]{1,3,2,0:T(8,128)(2,1)}, bf16[4,2...) while((s32[]{:T(128)}, ...), condition=%wide.region_17.18_spmd, body=%wide.region_13.17_spmd.sunk | while | flops 795121152 | bytes 42630428 | solution.py:266
  674.5 7.1 fusion.201
  681.6 4.2 fusion.200
  701.7 31.8 %reduce-scatter.11.cloned.1.call-done = bf16[512,768]{1,0:T(8,128)(2,1)} async-done(((bf16[2048,768]{1,0:T(8,128)(2,1)}), bf16[512,768]{1,0:T(8,128)(2,1)}) %reduce-scatter.11.cloned.1.call-update) | async-done | bytes 786448 | tf_op jit(solution)/shard_map/reduce_scatter | solution.py:290
  735.6 18.4 %all-reduce.2 = (f32[768]{0:T(1024)S(1)}, f32[768]{0:T(1024)S(1)}, f32[768]{0:T(1024)S(1)}, f32[768]{0:T(1024)S(1)}, f32[768]{0:T(1024)S(1)}, /*index=5*/f32[768]{0:T(1024)S(1)}) all-reduce(f32[768]{0:T(1024)S(1)} %get-tuple-element.260, f32[768]{0:T(1024)S(1)} %get-tuple-element.265, ...), channel_id=1, replica_groups=mesh['batch'=8,'head'=4] {'head'}, use_global_device_ids=true, to_apply=%region_22.23 | all-reduce | flops 4608 | bytes 36864 | tf_op jit(solution)/shard_map/psum | solution.py:341
  754.0 25.8 %all-reduce = (f32[768]{0:T(1024)}, f32[768]{0:T(1024)}, f32[192]{0:T(256)}, f32[192]{0:T(256)}, f32[768]{0:T(1024)}, /*index=5*/f32[768]{0:T(1024)}, f32[768]{0...) all-reduce(f32[768]{0:T(1024)S(1)} %get-tuple-element.345, ...), channel_id=1, replica_groups=mesh['batch'=8,'head'=4] {'batch'}, use_global_device_ids=true, to_apply=%region_23.24 | all-reduce | flops 7296 | bytes 58368 | tf_op jit(solution)/shard_map/psum | solution.py:340
  782.7 71.1 %all-reduce.5.cloned.1.call-done = (f32[768,192]{0,1:T(8,128)}, f32[768,192]{0,1:T(8,128)}, f32[768,192]{0,1:T(8,128)}, f32[192,768]{1,0:T(8,128)}, f32[768,768]{1,0:T(8,128)}, /*index=5*/f32[768,768]{1,0:T(8,128)}) async-done(((f32[768,192]{0,1:T(8,128)}, f32[768,192]{0,1:T(8,128)}, f32[768,192]{0,1:T(8,128)}, f32[192,768]{1,0:T(8,128)}, f32[768,768]{1,0:T(8,128)}, /*index=5*/f32[768,768]{1,0:T(8,128)}), ...) | async-done | bytes 7077904 | tf_op jit(solution)/shard_map/psum | solution.py:317
  (383 shorter events, 208.4 us)
Async XLA Ops:
  7.2 5.2 copy-start
  7.2 3.8 copy-start.1
  7.2 3.2 copy-start.47
  7.2 71.4 %all-gather.5.cloned.1.call-start = ((), (), s32[]{:S(2)}) async-start(), calls=%async_computation.4 | async-start | bytes 3932160 | tf_op jit(solution)/shard_map/all_gather | solution.py:189
  8.8 3.6 copy-start.51
  8.8 3.6 copy-start.52
  8.8 3.6 copy-start.53
  8.8 3.6 copy-start.26
  12.3 210.6 %reduce-scatter.5.cloned.1.call-start = ((), (), s32[]{:S(2)}) async-start(), calls=%async_computation.5 | async-start | bytes 3932160 | tf_op jit(solution)/shard_map/reduce_scatter | solution.py:225
  100.7 3.2 copy-start.34
  100.7 3.2 copy-start.54
  163.8 126.8 %all-gather.7.cloned.1.call-start = ((), (), s32[]{:S(2)}) async-start(), calls=%async_computation.6 | async-start | bytes 3932160 | tf_op jit(solution)/shard_map/all_gather | solution.py:234
  227.0 127.3 %all-gather.9.cloned.1.call-start = ((), (), s32[]{:S(2)}) async-start(), calls=%async_computation.8 | async-start | bytes 3932160 | tf_op jit(solution)/shard_map/all_gather | solution.py:245
  227.6 202.4 %reduce-scatter.9.cloned.1.call-start = ((), (), s32[]{:S(2)}) async-start(), calls=%async_computation.9 | async-start | bytes 3932160 | tf_op jit(solution)/shard_map/reduce_scatter | solution.py:252
  354.3 12.6 %copy-start.50 = (bf16[768,768]{1,0:T(8,128)(2,1)S(1)}, bf16[768,768]{1,0:T(8,128)(2,1)}, u32[]{:S(2)}) copy-start(bf16[768,768]{1,0:T(8,128)(2,1)} %param.41) | copy-start | bytes 3538948
  370.9 121.5 %reduce-scatter.7.cloned.1.call-start = ((), (), s32[]{:S(2)}) async-start(), calls=%async_computation.7 | async-start | bytes 3932160 | tf_op jit(solution)/shard_map/reduce_scatter | solution.py:237
  377.5 183.9 %all-gather.11.cloned.1.call-start = ((), (), s32[]{:S(2)}) async-start(), calls=%async_computation.10 | async-start | bytes 3932160 | tf_op jit(solution)/shard_map/all_gather | solution.py:262
  497.8 235.8 %reduce-scatter.11.cloned.1.call-start = ((), (), s32[]{:S(2)}) async-start(), calls=%async_computation.11 | async-start | bytes 3932160 | tf_op jit(solution)/shard_map/reduce_scatter | solution.py:290
  667.1 3.5 copy-start.9
  667.9 3.7 copy-start.12
  674.5 179.3 %all-reduce.5.cloned.1.call-start = ((), (), s32[]{:S(2)}) async-start(), calls=%async_computation.12 | async-start | bytes 14155776 | tf_op jit(solution)/shard_map/psum | solution.py:317
  674.5 7.1 copy-start.49
  674.5 7.1 copy-start.59
  681.6 4.2 copy-start.25
  695.3 6.1 copy-start.15
  695.3 38.3 %copy-start.36 = (f32[768]{0:T(1024)S(1)}, f32[768]{0:T(1024)}, u32[]{:S(2)}) copy-start(f32[768]{0:T(1024)} %copy-done.35) | copy-start | bytes 9220
  695.3 38.3 %copy-start.38 = (f32[512]{0:T(512)S(1)}, f32[512]{0:T(512)}, u32[]{:S(2)}) copy-start(f32[512]{0:T(512)} %copy-done.37) | copy-start | bytes 6148
  695.3 38.3 %copy-start.41 = (f32[512]{0:T(512)S(1)}, f32[512]{0:T(512)}, u32[]{:S(2)}) copy-start(f32[512]{0:T(512)} %copy-done.40) | copy-start | bytes 6148
  699.9 35.7 %copy-start.44 = (f32[768]{0:T(1024)S(1)}, f32[768]{0:T(1024)}, u32[]{:S(2)}) copy-start(f32[768]{0:T(1024)} %get-tuple-element.258) | copy-start | bytes 9220
  701.4 52.6 %copy-start.45 = (f32[192]{0:T(256)S(1)}, f32[192]{0:T(256)}, u32[]{:S(2)}) copy-start(f32[192]{0:T(256)} %reduce_sum.229) | copy-start | bytes 2308
  733.6 46.3 %copy-start.18 = (bf16[512,768]{1,0:T(8,128)(2,1)S(1)}, bf16[512,768]{1,0:T(8,128)(2,1)}, u32[]{:S(2)}) copy-start(bf16[512,768]{1,0:T(8,128)(2,1)} %reduce-scatter.11.cloned.1.call-done) | copy-start | bytes 2359300
  853.8 3.7 copy-start.22
  (43 other events, 79.4 us)
Sparse Core Ops, SparseCore 0:
  12.4 66.1 all-gather.4
  164.0 58.8 reduce-scatter.4
  227.1 63.5 all-gather.6
  292.1 62.1 all-gather.8
  371.0 58.8 reduce-scatter.8
  432.1 60.2 reduce-scatter.6
  497.9 63.5 all-gather.10
  674.6 58.8 reduce-scatter.10
  738.8 114.9 all-reduce.4
